TPU v7x, 256 devices: a whole 4x4x8 slice. The times are simulated.
256 devices in a mesh: wide: 32 (over y, x, core), narrow: 8 (over z).
Axes of the slice: x: 4, y: 4, z: 8, core: 2. Of those that a mesh axis runs over, the one named last changes fastest.
Arguments:
- features: bfloat16 [1024, 16384], P('wide', 'narrow'), may hold values from -6 to 6
- queries: bfloat16 [2048, 16384], P('wide', 'narrow'), may hold values from -6 to 6
- damping: float32 [16384], P('wide'), may hold values from 0.25 to 4
Outputs:
- kernel: float32 [16384, 16384], P('wide', 'narrow')
- factor: float32 [16384, 256], P('wide')
- scores: float32 [2048, 1024], P('wide', 'narrow')
All inputs are finite; a program needn't handle non-finite values.
Results may differ from a plain program's by a relative error of at most 0.0003.
Values may be sent and summed in bfloat16 or wider, within the bound.
A program may use at most 64 MiB of HBM per device.

v0:
```python
import math
import jax
import jax.numpy as jnp
from jax import lax
from jax.sharding import PartitionSpec as P

P_SIZE = 16384
PANEL = 128
PANELS = 2


def laid_out(pieces, dim):
    pieces = jnp.moveaxis(pieces, 0, dim)
    shape = pieces.shape
    return pieces.reshape(*shape[:dim], shape[dim] * shape[dim + 1], *shape[dim + 2 :])


def copy_for_each(x, axis):
    copies = jnp.broadcast_to(x, (lax.axis_size(axis), *x.shape))
    return lax.all_to_all(copies, axis, split_axis=0, concat_axis=0, tiled=True)


def collect(x, axis, dim):
    return laid_out(copy_for_each(x, axis), dim)


def in_blocks(x, dim, size):
    before, after = (x.shape[:dim], x.shape[dim + 1 :])
    return jnp.moveaxis(x.reshape(*before, size, -1, *after), dim, 0)


def sent_and_summed(x, axis, dim):
    size = lax.axis_size(axis)
    pieces = lax.all_to_all(in_blocks(x, dim, size), axis, 0, 0, tiled=True)
    return jnp.sum(pieces, axis=0)


def broadcast(x, axis, root):
    return lax.dynamic_index_in_dim(lax.all_gather(x, axis), root, 0, keepdims=False)


def on_device(features, queries, damping):
    rows_here = damping.shape[0]
    cols_here = queries.shape[1]
    slab_total = features.shape[0] * lax.axis_size("wide")
    wide_pos = lax.axis_index("wide")
    narrow_pos = lax.axis_index("narrow")
    contract_rows = (((0,), (0,)), ((), ()))
    contract_cols = (((1,), (1,)), ((), ()))
    full_width = collect(features, "narrow", 1)
    row_features = lax.all_to_all(full_width, "wide", split_axis=1, concat_axis=0, tiled=True)
    slab_columns = lax.all_gather(features, "wide", axis=0, tiled=True)
    products = lax.dot_general(
        row_features, slab_columns, contract_rows, preferred_element_type=jnp.float32
    )
    partial_value = lax.dot_general(
        queries, slab_columns, contract_cols, preferred_element_type=jnp.float32
    )
    scores = sent_and_summed(partial_value, "narrow", 1) * (1.0 / math.sqrt(P_SIZE))
    row_ids = wide_pos * rows_here + lax.broadcasted_iota(jnp.int32, (rows_here, 1), 0)
    col_ids = narrow_pos * cols_here + lax.broadcasted_iota(jnp.int32, (1, cols_here), 1)
    kernel_block = products / slab_total + jnp.where(
        row_ids == col_ids, damping[:, None], jnp.float32(0.0)
    )
    factors = []
    for panel_index in range(PANELS):
        offset = panel_index * PANEL
        column_root = offset // cols_here
        row_root = offset // rows_here
        col_shift = offset % cols_here
        row_shift = offset % rows_here
        panel_columns = broadcast(
            kernel_block[:, col_shift : col_shift + PANEL], "narrow", column_root
        )
        pivot_block = broadcast(panel_columns[row_shift : row_shift + PANEL], "wide", row_root)
        pivot_factor = jnp.linalg.cholesky(pivot_block)
        lower_rows = lax.linalg.triangular_solve(
            pivot_factor, panel_columns, left_side=False, lower=True, transpose_a=True
        )
        per_group = cols_here // rows_here
        pieces = []
        for member in range(per_group):
            pieces.append(broadcast(lower_rows, "wide", narrow_pos * per_group + member))
        lower_cols = jnp.concatenate(pieces, axis=0)
        kernel_block = kernel_block - jnp.dot(
            lower_rows,
            lower_cols.T,
            precision=lax.Precision.HIGHEST,
            preferred_element_type=jnp.float32,
        )
        boundary = offset + PANEL
        kernel_block = jnp.where(
            (row_ids < boundary) | (col_ids < boundary), jnp.zeros_like(kernel_block), kernel_block
        )
        factors.append(lower_rows)
    return (kernel_block, jnp.concatenate(factors, axis=1), scores)


def solution(mesh):
    return jax.shard_map(
        on_device,
        mesh=mesh,
        in_specs=(P("wide", "narrow"), P("wide", "narrow"), P("wide")),
        out_specs=(P("wide", "narrow"), P("wide", None), P("wide", "narrow")),
        check_vma=False,
    )
```

profile of v0, /device:TPU:1, one launch (start us, length us, event | category | flops | bytes accessed | tf_op | source)
XLA Modules:
  0.0 475.1 jit_solution(2787711246564530403)
XLA Ops:
  7.2 0.7 all-gather.12.cloned.1.call-update
  7.9 1.0 broadcast_in_dim.15
  8.9 36.2 %all_to_all.29 = bf16[8,32,2048]{2,1,0:T(8,128)(2,1)S(1)} all-to-all(bf16[8,32,2048]{2,1,0:T(8,128)(2,1)S(1)} %broadcast_in_dim.15), channel_id=1, replica_groups=mesh['wide'=32,'narrow'=8] {'narrow'}, dimensions={0} | all-to-all | bytes 2097152 | tf_op jit(solution)/shard_map/all_to_all | solution.py:20
  45.7 0.7 all_to_all.21
  46.4 1.5 copy.16
  47.9 9.4 %all-to-all-start.1 = ((bf16[32,32,512]{2,0,1:T(8,128)(2,1)}), bf16[32,32,512]{2,0,1:T(8,128)(2,1)S(1)}, u32[]{:S(2)}, u32[]{:S(2)}) async-start(bf16[32,32,512]{2,0,1:T(8,128)(2,1)} %copy.16), calls=%async_computation.1 | async-start | bytes 2097152 | tf_op jit(solution)/shard_map/all_to_all | solution.py:51
  57.4 18.8 %all-to-all-done.1 = bf16[32,32,512]{2,0,1:T(8,128)(2,1)S(1)} async-done(((bf16[32,32,512]{2,0,1:T(8,128)(2,1)}), bf16[32,32,512]{2,0,1:T(8,128)(2,1)S(1)}, u32[]{:S(2)}, u32[]{:S(2)}) %all-to-all-start.1) | async-done | bytes 1048608 | tf_op jit(solution)/shard_map/all_to_all | solution.py:51
  76.2 5.0 %select_add_fusion = f32[512,2048]{1,0:T(8,128)S(1)} fusion(bf16[1024,512]{1,0:T(8,128)(2,1)S(1)} %bitcast.87, bf16[1024,2048]{1,0:T(8,128)(2,1)} %all-gather.12.cloned.1.call-done, f32[512]{0:T(512)S(1)} %copy-done.7, s32[2048]{0:T(1024)S(1)} %iota_add_fusion, s32[512]{0:T(512)S(1)} %iota_add_fusion.1), kind=kOutput, calls=%fused_computation.2 | convolution fusion | flops 2151677952 | bytes 9449472 | tf_op jit(solution)/shard_map/dot_general | solution.py:53
  81.2 2.0 copy-done.3
  83.2 0.7 slice.32
  84.0 33.5 %all-gather.18.cloned.1.call-done = f32[4096,128]{1,0:T(8,128)} async-done(((f32[512,128]{1,0:T(8,128)}), f32[4096,128]{1,0:T(8,128)}) %all-gather.18.cloned.1.call-update) | async-done | bytes 2097168 | tf_op jit(solution)/shard_map/all_gather | solution.py:39
  117.6 1.5 slice.33
  119.1 53.3 %all-gather.14.cloned.1.call-done = f32[32,128,128]{2,1,0:T(8,128)} async-done(((f32[1,128,128]{2,1,0:T(8,128)}), f32[32,128,128]{2,1,0:T(8,128)}) %all-gather.14.cloned.1.call-update) | async-done | bytes 2097168 | tf_op jit(solution)/shard_map/all_gather | solution.py:39
  172.5 0.8 dynamic_slice.51
  173.4 0.9 fusion.19
  174.2 11.7 %cholesky.44 = f32[128,128]{1,0:T(8,128)S(1)} custom-call(f32[128,128]{1,0:T(8,128)S(1)} %fusion.19), custom_call_target="Cholesky" | custom-call | tf_op jit(solution)/shard_map/jit(cholesky)/cholesky | solution.py:76
  186.0 0.6 compare_reduce_fusion.1
  186.6 0.7 fusion.16
  187.3 9.8 %custom-call.6 = f32[1,128,128]{1,2,0:T(8,128)S(1)} custom-call(f32[1,128,128]{2,1,0:T(8,128)S(1)} %fusion.16), custom_call_target="InvertDiagBlocksLowerTriangular" | custom-call | tf_op jit(solution)/shard_map/triangular_solve/custom-call.0 | solution.py:77
  197.1 2.1 convolution_bitcast_fusion.2
  199.8 56.8 %all-gather.20.cloned.1.call-done = f32[16384,128]{0,1:T(8,128)} async-done(((f32[512,128]{0,1:T(8,128)}), f32[16384,128]{0,1:T(8,128)}) %all-gather.20.cloned.1.call-update) | async-done | bytes 8388624 | tf_op jit(solution)/shard_map/all_gather | solution.py:39
  256.6 9.9 %copy.36 = f32[16,8,32,512]{3,2,1,0:T(8,128)S(1)} copy(f32[16,8,32,512]{3,1,2,0:T(8,128)} %bitcast.80) | data formatting | bytes 16777216
  266.5 1.2 constant_dynamic-slice_fusion.7
  267.8 0.9 copy-done.4
  268.7 4.1 subtract_select_fusion.1
  272.8 2.0 copy-done.1
  274.8 0.7 slice.35
  275.6 36.0 %all-gather.22.cloned.1.call-done = f32[4096,128]{1,0:T(8,128)} async-done(((f32[512,128]{1,0:T(8,128)}), f32[4096,128]{1,0:T(8,128)}) %all-gather.22.cloned.1.call-update) | async-done | bytes 2097168 | tf_op jit(solution)/shard_map/all_gather | solution.py:39
  311.6 1.5 slice.36
  313.3 53.0 %all-gather.16.cloned.1.call-done = f32[32,128,128]{2,1,0:T(8,128)} async-done(((f32[1,128,128]{2,1,0:T(8,128)}), f32[32,128,128]{2,1,0:T(8,128)}) %all-gather.16.cloned.1.call-update) | async-done | bytes 2097168 | tf_op jit(solution)/shard_map/all_gather | solution.py:39
  366.3 0.8 dynamic_slice.52
  367.3 0.9 fusion.18
  368.1 11.7 %cholesky.55 = f32[128,128]{1,0:T(8,128)S(1)} custom-call(f32[128,128]{1,0:T(8,128)S(1)} %fusion.18), custom_call_target="Cholesky" | custom-call | tf_op jit(solution)/shard_map/jit(cholesky)/cholesky | solution.py:76
  379.9 0.6 compare_reduce_fusion
  380.5 0.7 fusion.17
  381.2 9.8 %custom-call.7 = f32[1,128,128]{1,2,0:T(8,128)S(1)} custom-call(f32[1,128,128]{2,1,0:T(8,128)S(1)} %fusion.17), custom_call_target="InvertDiagBlocksLowerTriangular" | custom-call | tf_op jit(solution)/shard_map/triangular_solve/custom-call.0 | solution.py:77
  391.0 2.1 convolution_bitcast_fusion.1
  393.1 3.6 convolution_bitcast_fusion
  396.8 0.7 copy.47
  397.5 7.0 %all-to-all-start.2 = ((f32[8,64,128]{2,1,0:T(8,128)}), f32[8,64,128]{2,1,0:T(8,128)S(1)}, u32[]{:S(2)}, u32[]{:S(2)}) async-start(f32[8,64,128]{2,1,0:T(8,128)} %bitcast.73), calls=%async_computation.2 | async-start | bytes 524288 | tf_op jit(solution)/shard_map/all_to_all | solution.py:34
  404.5 11.6 %all-to-all-done.2 = f32[8,64,128]{2,1,0:T(8,128)S(1)} async-done(((f32[8,64,128]{2,1,0:T(8,128)}), f32[8,64,128]{2,1,0:T(8,128)S(1)}, u32[]{:S(2)}, u32[]{:S(2)}) %all-to-all-start.2) | async-done | bytes 262176 | tf_op jit(solution)/shard_map/all_to_all | solution.py:34
  416.2 0.6 broadcast_multiply_fusion
  416.8 1.0 copy.22
  417.8 32.7 %all-gather.24.cloned.1.call-done = f32[16384,128]{0,1:T(8,128)} async-done(((f32[512,128]{0,1:T(8,128)}), f32[16384,128]{0,1:T(8,128)}) %all-gather.24.cloned.1.call-update) | async-done | bytes 8388624 | tf_op jit(solution)/shard_map/all_gather | solution.py:39
  450.5 9.9 %copy.37 = f32[16,8,32,512]{3,2,1,0:T(8,128)S(1)} copy(f32[16,8,32,512]{3,1,2,0:T(8,128)} %bitcast.81) | data formatting | bytes 16777216
  460.4 1.2 constant_dynamic-slice_fusion.3
  461.7 0.9 copy-done.2
  462.6 5.5 %subtract_select_fusion = f32[512,2048]{1,0:T(8,128)} fusion(f32[512,2048]{1,0:T(8,128)S(1)} %copy-done.2, f32[512,128]{0,1:T(8,128)S(1)} %copy-done.6, pred[2048]{0:T(1024)(128)(4,1)S(1)} %fusion.23, pred[512]{0:T(512)(128)(4,1)S(1)} %fusion.25, f32[512,128]{0,1:T(8,128)S(1)} %bitcast.84, f32[512,128]{0,1:T(8,128)S(1)} %bitcast.85, ...), kind=kOutput, calls=%fused_computation | convolution fusion | flops 1614544896 | bytes 9701888 | tf_op jit(solution)/shard_map/dot_general | solution.py:85
  (45 shorter events, 2.1 us)
Async XLA Ops:
  7.2 386.0 %copy-start = (bf16[64,2048]{1,0:T(8,128)(2,1)S(1)}, bf16[64,2048]{1,0:T(8,128)(2,1)}, u32[]{:S(2)}) copy-start(bf16[64,2048]{1,0:T(8,128)(2,1)} %param.7) | copy-start | bytes 786436
  7.2 69.1 %all-gather.12.cloned.1.call-start = ((), (), s32[]{:S(2)}) async-start(), calls=%async_computation.3 | async-start | bytes 4325376 | tf_op jit(solution)/shard_map/all_gather | solution.py:52
  45.1 31.2 %copy-start.7 = (f32[512]{0:T(512)S(1)}, f32[512]{0:T(512)}, u32[]{:S(2)}) copy-start(f32[512]{0:T(512)} %param.8) | copy-start | bytes 6148
  47.9 28.3 %all-to-all-start.1 = ((bf16[32,32,512]{2,0,1:T(8,128)(2,1)}), bf16[32,32,512]{2,0,1:T(8,128)(2,1)S(1)}, u32[]{:S(2)}, u32[]{:S(2)}) async-start(bf16[32,32,512]{2,0,1:T(8,128)(2,1)} %copy.16), calls=%async_computation.1 | async-start | bytes 2097152 | tf_op jit(solution)/shard_map/all_to_all | solution.py:51
  57.3 60.2 %all-gather.18.cloned.1.call-start = ((), (), s32[]{:S(2)}) async-start(), calls=%async_computation.6 | async-start | bytes 2359296 | tf_op jit(solution)/shard_map/all_gather | solution.py:39
  81.2 2.0 copy-start.3
  84.0 88.5 %all-gather.14.cloned.1.call-start = ((), (), s32[]{:S(2)}) async-start(), calls=%async_computation.4 | async-start | bytes 2162688 | tf_op jit(solution)/shard_map/all_gather | solution.py:39
  119.1 137.5 %all-gather.20.cloned.1.call-start = ((), (), s32[]{:S(2)}) async-start(), calls=%async_computation.7 | async-start | bytes 8650752 | tf_op jit(solution)/shard_map/all_gather | solution.py:39
  199.2 112.4 %all-gather.22.cloned.1.call-start = ((), (), s32[]{:S(2)}) async-start(), calls=%async_computation.8 | async-start | bytes 2359296 | tf_op jit(solution)/shard_map/all_gather | solution.py:39
  256.6 11.2 %copy-start.5 = (f32[512,128]{0,1:T(8,128)S(1)}, f32[512,128]{0,1:T(8,128)}, u32[]{:S(2)}) copy-start(f32[512,128]{0,1:T(8,128)} %convolution_bitcast_fusion.2) | copy-start | bytes 786436
  266.5 2.2 copy-start.4
  272.8 2.0 copy-start.1
  275.5 90.8 %all-gather.16.cloned.1.call-start = ((), (), s32[]{:S(2)}) async-start(), calls=%async_computation.5 | async-start | bytes 2162688 | tf_op jit(solution)/shard_map/all_gather | solution.py:39
  313.1 137.4 %all-gather.24.cloned.1.call-start = ((), (), s32[]{:S(2)}) async-start(), calls=%async_computation.9 | async-start | bytes 8650752 | tf_op jit(solution)/shard_map/all_gather | solution.py:39
  393.1 23.7 %copy-start.6 = (f32[512,128]{0,1:T(8,128)S(1)}, f32[512,128]{0,1:T(8,128)}, u32[]{:S(2)}) copy-start(f32[512,128]{0,1:T(8,128)} %convolution_bitcast_fusion.1) | copy-start | bytes 786436
  397.5 18.6 %all-to-all-start.2 = ((f32[8,64,128]{2,1,0:T(8,128)}), f32[8,64,128]{2,1,0:T(8,128)S(1)}, u32[]{:S(2)}, u32[]{:S(2)}) async-start(f32[8,64,128]{2,1,0:T(8,128)} %bitcast.73), calls=%async_computation.2 | async-start | bytes 524288 | tf_op jit(solution)/shard_map/all_to_all | solution.py:34
  460.4 2.2 copy-start.2
Sparse Core Ops, SparseCore 0:
  10.5 60.5 all-gather.11
  84.1 33.4 all-gather.17
  120.7 51.7 all-gather.13
  199.3 57.1 all-gather.19
  275.7 35.8 all-gather.21
  314.6 51.7 all-gather.15
  393.3 57.1 all-gather.23
where the time goes:
time: 484 us; the launch traced here: 475 us
  waiting for transfers between devices  297 us (61%)
  other arithmetic  48.1 us (10%)
  local copies, waits for them, and re-layouts  39.9 us (8%)
  blocking collectives  36.2 us (7%)
  matrix products  22.3 us (5%)
  starting transfers between devices  17.3 us (4%)
  between operations  14.6 us (3%)
    all_gather x6, waiting for transfers between devices, broadcast(): lax.all_gather(x, axis)  265 us
    all_to_all x1, blocking collectives, copy_for_each(): return lax.all_to_all(copies, axis, split_axis=0, concat_axis=0, tiled=True)  36.2 us
    unnamed x27, local copies, waits for them, and re-layouts  26.9 us
    another operation x6, other arithmetic, on_device(): pivot_factor = jnp.linalg.cholesky(pivot_block)  24.8 us
    another operation x4, other arithmetic, on_device(): lax.linalg.triangular_solve(pivot_factor, panel_columns, left_side=False,...  20.9 us
    all_to_all x1, waiting for transfers between devices, on_device(): lax.all_to_all(full_width, 'wide', split_axis=1, concat_axis=0, tiled=True)  18.8 us
    all_to_all x1, waiting for transfers between devices, sent_and_summed(): pieces = lax.all_to_all(in_blocks(x, dim, size), axis, 0, 0, tiled=True)  11.6 us
  transfers between devices with their start and end apart: 9, of which 8 were waited for; matrix products, arithmetic and copies ran while one was open for 2% of the time, Pallas kernels for 0%

commit v1 on v0

--- a/solution.py
+++ b/solution.py
@@ -48,7 +48,9 @@
     contract_rows = (((0,), (0,)), ((), ()))
     contract_cols = (((1,), (1,)), ((), ()))
     full_width = collect(features, "narrow", 1)
-    row_features = lax.all_to_all(full_width, "wide", split_axis=1, concat_axis=0, tiled=True)
+    parts = jnp.split(full_width, lax.axis_size("wide"), axis=1)
+    incoming = lax.all_to_all(jnp.stack(parts), "wide", 0, 0)
+    row_features = jnp.concatenate(incoming, axis=0)
     slab_columns = lax.all_gather(features, "wide", axis=0, tiled=True)
     products = lax.dot_general(
         row_features, slab_columns, contract_rows, preferred_element_type=jnp.float32

time: 484 us -> 495 us (1.023)
  blocking collectives: 36.2 us -> 0 us
  waiting for transfers between devices: 297 us -> 319 us
  local copies, waits for them, and re-layouts: 39.9 us -> 58 us
  starting transfers between devices: 17.3 us -> 24.6 us
    all_to_all x1 -> x0, blocking collectives: 36.2 us -> none  [copy_for_each(): return lax.all_to_all(copies, axis, split_axis=0, concat_axis=0, tiled=True)]
    all_to_all x1 -> x2, waiting for transfers between devices: 18.8 us -> 45.4 us  [the longest x1 28.5 us: copy_for_each(): return lax.all_to_all(copies, axis, split_axis=0, concat_axis=0, tiled=True)]
    unnamed x27 -> x58, local copies, waits for them, and re-layouts: 26.9 us -> 46.1 us
    all_to_all x1 -> x2, starting transfers between devices: 9.42 us -> 16.7 us  [the longest x1 9.13 us: copy_for_each(): return lax.all_to_all(copies, axis, split_axis=0, concat_axis=0, tiled=True)]
  transfers between devices with their start and end apart: 9 -> 10, of which waited for: 8 -> 9; matrix products, arithmetic and copies ran while one was open for 2% -> 5% of each run, Pallas kernels for 0% -> 0%
where the time goes in v1:
time: 495 us; the launch traced here: 487 us
  waiting for transfers between devices  319 us (64%)
  local copies, waits for them, and re-layouts  58 us (12%)
  other arithmetic  48.1 us (10%)
  starting transfers between devices  24.6 us (5%)
  matrix products  22.3 us (5%)
  between operations  14.7 us (3%)
    all_gather x6, waiting for transfers between devices, broadcast(): lax.all_gather(x, axis)  261 us
    unnamed x58, local copies, waits for them, and re-layouts  46.1 us
    all_to_all x1, waiting for transfers between devices, copy_for_each(): return lax.all_to_all(copies, axis, split_axis=0, concat_axis=0, tiled=True)  28.5 us
    another operation x6, other arithmetic, on_device(): pivot_factor = jnp.linalg.cholesky(pivot_block)  24.8 us
    another operation x4, other arithmetic, on_device(): lax.linalg.triangular_solve(pivot_factor, panel_columns, left_side=False,...  20.9 us
    all_to_all x1, waiting for transfers between devices, on_device(): incoming = lax.all_to_all(jnp.stack(parts), 'wide', 0, 0)  17 us
    all_to_all x1, waiting for transfers between devices, sent_and_summed(): pieces = lax.all_to_all(in_blocks(x, dim, size), axis, 0, 0, tiled=True)  11.6 us
  transfers between devices with their start and end apart: 10, of which 9 were waited for; matrix products, arithmetic and copies ran while one was open for 5% of the time, Pallas kernels for 0%

profile of v1, /device:TPU:1, one launch (start us, length us, event | category | flops | bytes accessed | tf_op | source)
XLA Modules:
  0.0 486.7 jit_solution(17475636749044794800)
XLA Ops:
  7.2 2.0 broadcast_in_dim.15
  9.2 9.1 %all-to-all-start = ((bf16[8,32,2048]{2,1,0:T(8,128)(2,1)}), bf16[8,32,2048]{2,1,0:T(8,128)(2,1)S(1)}, u32[]{:S(2)}, u32[]{:S(2)}) async-start(bf16[8,32,2048]{2,1,0:T(8,128)(2,1)} %broadcast_in_dim.15), calls=%async_computation | async-start | bytes 2097152 | tf_op jit(solution)/shard_map/all_to_all | solution.py:20
  18.4 0.7 all-gather.12.cloned.1.call-update
  19.1 28.5 %all-to-all-done = bf16[8,32,2048]{2,1,0:T(8,128)(2,1)S(1)} async-done(((bf16[8,32,2048]{2,1,0:T(8,128)(2,1)}), bf16[8,32,2048]{2,1,0:T(8,128)(2,1)S(1)}, u32[]{:S(2)}, u32[]{:S(2)}) %all-to-all-start) | async-done | bytes 1048608 | tf_op jit(solution)/shard_map/all_to_all | solution.py:20
  47.7 0.6 constant_dynamic-update-slice_fusion.31
  67.4 7.6 %all-to-all-start.1 = ((bf16[32,32,512]{2,1,0:T(8,128)(2,1)}), bf16[32,32,512]{2,1,0:T(8,128)(2,1)S(1)}, u32[]{:S(2)}, u32[]{:S(2)}) async-start(bf16[32,32,512]{2,1,0:T(8,128)(2,1)} %constant_dynamic-update-slice_fusion), calls=%async_computation.1 | async-start | bytes 2097152 | tf_op jit(solution)/shard_map/all_to_all | solution.py:52
  75.1 17.0 %all-to-all-done.1 = bf16[32,32,512]{2,1,0:T(8,128)(2,1)S(1)} async-done(((bf16[32,32,512]{2,1,0:T(8,128)(2,1)}), bf16[32,32,512]{2,1,0:T(8,128)(2,1)S(1)}, u32[]{:S(2)}, u32[]{:S(2)}) %all-to-all-start.1) | async-done | bytes 1048608 | tf_op jit(solution)/shard_map/all_to_all | solution.py:52
  92.0 5.0 %select_add_fusion = f32[512,2048]{1,0:T(8,128)S(1)} fusion(bf16[1024,512]{1,0:T(8,128)(2,1)S(1)} %bitcast.247, bf16[1024,2048]{1,0:T(8,128)(2,1)} %all-gather.12.cloned.1.call-done, f32[512]{0:T(512)S(1)} %copy-done.7, s32[2048]{0:T(1024)S(1)} %iota_add_fusion, s32[512]{0:T(512)S(1)} %iota_add_fusion.1), kind=kOutput, calls=%fused_computation.2 | convolution fusion | flops 2151677952 | bytes 9449472 | tf_op jit(solution)/shard_map/dot_general | solution.py:55
  97.0 2.0 copy-done.3
  99.0 0.7 slice.32
  99.8 29.3 %all-gather.18.cloned.1.call-done = f32[4096,128]{1,0:T(8,128)} async-done(((f32[512,128]{1,0:T(8,128)}), f32[4096,128]{1,0:T(8,128)}) %all-gather.18.cloned.1.call-update) | async-done | bytes 2097168 | tf_op jit(solution)/shard_map/all_gather | solution.py:39
  129.2 1.5 slice.33
  130.7 53.3 %all-gather.14.cloned.1.call-done = f32[32,128,128]{2,1,0:T(8,128)} async-done(((f32[1,128,128]{2,1,0:T(8,128)}), f32[32,128,128]{2,1,0:T(8,128)}) %all-gather.14.cloned.1.call-update) | async-done | bytes 2097168 | tf_op jit(solution)/shard_map/all_gather | solution.py:39
  184.1 0.8 dynamic_slice.51
  185.0 0.9 fusion.19
  185.9 11.7 %cholesky.44 = f32[128,128]{1,0:T(8,128)S(1)} custom-call(f32[128,128]{1,0:T(8,128)S(1)} %fusion.19), custom_call_target="Cholesky" | custom-call | tf_op jit(solution)/shard_map/jit(cholesky)/cholesky | solution.py:78
  197.6 0.6 compare_reduce_fusion.1
  198.3 0.7 fusion.16
  198.9 9.8 %custom-call.6 = f32[1,128,128]{1,2,0:T(8,128)S(1)} custom-call(f32[1,128,128]{2,1,0:T(8,128)S(1)} %fusion.16), custom_call_target="InvertDiagBlocksLowerTriangular" | custom-call | tf_op jit(solution)/shard_map/triangular_solve/custom-call.0 | solution.py:79
  208.7 2.1 convolution_bitcast_fusion.2
  211.4 56.8 %all-gather.20.cloned.1.call-done = f32[16384,128]{0,1:T(8,128)} async-done(((f32[512,128]{0,1:T(8,128)}), f32[16384,128]{0,1:T(8,128)}) %all-gather.20.cloned.1.call-update) | async-done | bytes 8388624 | tf_op jit(solution)/shard_map/all_gather | solution.py:39
  268.2 9.9 %copy.35 = f32[16,8,32,512]{3,2,1,0:T(8,128)S(1)} copy(f32[16,8,32,512]{3,1,2,0:T(8,128)} %bitcast.208) | data formatting | bytes 16777216
  278.1 1.2 constant_dynamic-slice_fusion.7
  279.4 0.9 copy-done.4
  280.3 4.1 subtract_select_fusion.1
  284.4 2.0 copy-done.1
  286.4 0.7 slice.35
  287.2 36.0 %all-gather.22.cloned.1.call-done = f32[4096,128]{1,0:T(8,128)} async-done(((f32[512,128]{1,0:T(8,128)}), f32[4096,128]{1,0:T(8,128)}) %all-gather.22.cloned.1.call-update) | async-done | bytes 2097168 | tf_op jit(solution)/shard_map/all_gather | solution.py:39
  323.2 1.5 slice.36
  324.9 53.0 %all-gather.16.cloned.1.call-done = f32[32,128,128]{2,1,0:T(8,128)} async-done(((f32[1,128,128]{2,1,0:T(8,128)}), f32[32,128,128]{2,1,0:T(8,128)}) %all-gather.16.cloned.1.call-update) | async-done | bytes 2097168 | tf_op jit(solution)/shard_map/all_gather | solution.py:39
  378.0 0.8 dynamic_slice.52
  378.9 0.9 fusion.18
  379.8 11.7 %cholesky.55 = f32[128,128]{1,0:T(8,128)S(1)} custom-call(f32[128,128]{1,0:T(8,128)S(1)} %fusion.18), custom_call_target="Cholesky" | custom-call | tf_op jit(solution)/shard_map/jit(cholesky)/cholesky | solution.py:78
  391.5 0.6 compare_reduce_fusion
  392.2 0.7 fusion.17
  392.8 9.8 %custom-call.7 = f32[1,128,128]{1,2,0:T(8,128)S(1)} custom-call(f32[1,128,128]{2,1,0:T(8,128)S(1)} %fusion.17), custom_call_target="InvertDiagBlocksLowerTriangular" | custom-call | tf_op jit(solution)/shard_map/triangular_solve/custom-call.0 | solution.py:79
  402.6 2.1 convolution_bitcast_fusion.1
  404.8 3.6 convolution_bitcast_fusion
  408.4 0.7 copy.46
  409.1 7.0 %all-to-all-start.2 = ((f32[8,64,128]{2,1,0:T(8,128)}), f32[8,64,128]{2,1,0:T(8,128)S(1)}, u32[]{:S(2)}, u32[]{:S(2)}) async-start(f32[8,64,128]{2,1,0:T(8,128)} %bitcast.201), calls=%async_computation.2 | async-start | bytes 524288 | tf_op jit(solution)/shard_map/all_to_all | solution.py:34
  416.1 11.6 %all-to-all-done.2 = f32[8,64,128]{2,1,0:T(8,128)S(1)} async-done(((f32[8,64,128]{2,1,0:T(8,128)}), f32[8,64,128]{2,1,0:T(8,128)S(1)}, u32[]{:S(2)}, u32[]{:S(2)}) %all-to-all-start.2) | async-done | bytes 262176 | tf_op jit(solution)/shard_map/all_to_all | solution.py:34
  427.8 0.6 broadcast_multiply_fusion
  428.4 1.0 copy.20
  429.4 32.7 %all-gather.24.cloned.1.call-done = f32[16384,128]{0,1:T(8,128)} async-done(((f32[512,128]{0,1:T(8,128)}), f32[16384,128]{0,1:T(8,128)}) %all-gather.24.cloned.1.call-update) | async-done | bytes 8388624 | tf_op jit(solution)/shard_map/all_gather | solution.py:39
  462.1 9.9 %copy.36 = f32[16,8,32,512]{3,2,1,0:T(8,128)S(1)} copy(f32[16,8,32,512]{3,1,2,0:T(8,128)} %bitcast.209) | data formatting | bytes 16777216
  472.0 1.2 constant_dynamic-slice_fusion.3
  473.3 0.9 copy-done.2
  474.2 5.5 %subtract_select_fusion = f32[512,2048]{1,0:T(8,128)} fusion(f32[512,2048]{1,0:T(8,128)S(1)} %copy-done.2, f32[512,128]{0,1:T(8,128)S(1)} %copy-done.6, pred[2048]{0:T(1024)(128)(4,1)S(1)} %fusion.23, pred[512]{0:T(512)(128)(4,1)S(1)} %fusion.25, f32[512,128]{0,1:T(8,128)S(1)} %bitcast.244, f32[512,128]{0,1:T(8,128)S(1)} %bitcast.245, ...), kind=kOutput, calls=%fused_computation | convolution fusion | flops 1614544896 | bytes 9701888 | tf_op jit(solution)/shard_map/dot_general | solution.py:87
  (76 shorter events, 20.8 us)
Async XLA Ops:
  7.2 397.6 %copy-start = (bf16[64,2048]{1,0:T(8,128)(2,1)S(1)}, bf16[64,2048]{1,0:T(8,128)(2,1)}, u32[]{:S(2)}) copy-start(bf16[64,2048]{1,0:T(8,128)(2,1)} %param.7) | copy-start | bytes 786436
  9.2 82.8 %copy-start.7 = (f32[512]{0:T(512)S(1)}, f32[512]{0:T(512)}, u32[]{:S(2)}) copy-start(f32[512]{0:T(512)} %param.8) | copy-start | bytes 6148
  9.2 38.3 %all-to-all-start = ((bf16[8,32,2048]{2,1,0:T(8,128)(2,1)}), bf16[8,32,2048]{2,1,0:T(8,128)(2,1)S(1)}, u32[]{:S(2)}, u32[]{:S(2)}) async-start(bf16[8,32,2048]{2,1,0:T(8,128)(2,1)} %broadcast_in_dim.15), calls=%async_computation | async-start | bytes 2097152 | tf_op jit(solution)/shard_map/all_to_all | solution.py:20
  18.4 73.7 %all-gather.12.cloned.1.call-start = ((), (), s32[]{:S(2)}) async-start(), calls=%async_computation.3 | async-start | bytes 4325376 | tf_op jit(solution)/shard_map/all_gather | solution.py:54
  67.4 24.6 %all-to-all-start.1 = ((bf16[32,32,512]{2,1,0:T(8,128)(2,1)}), bf16[32,32,512]{2,1,0:T(8,128)(2,1)S(1)}, u32[]{:S(2)}, u32[]{:S(2)}) async-start(bf16[32,32,512]{2,1,0:T(8,128)(2,1)} %constant_dynamic-update-slice_fusion), calls=%async_computation.1 | async-start | bytes 2097152 | tf_op jit(solution)/shard_map/all_to_all | solution.py:52
  75.0 54.2 %all-gather.18.cloned.1.call-start = ((), (), s32[]{:S(2)}) async-start(), calls=%async_computation.6 | async-start | bytes 2359296 | tf_op jit(solution)/shard_map/all_gather | solution.py:39
  97.0 2.0 copy-start.3
  99.8 84.3 %all-gather.14.cloned.1.call-start = ((), (), s32[]{:S(2)}) async-start(), calls=%async_computation.4 | async-start | bytes 2162688 | tf_op jit(solution)/shard_map/all_gather | solution.py:39
  130.7 137.5 %all-gather.20.cloned.1.call-start = ((), (), s32[]{:S(2)}) async-start(), calls=%async_computation.7 | async-start | bytes 8650752 | tf_op jit(solution)/shard_map/all_gather | solution.py:39
  210.8 112.4 %all-gather.22.cloned.1.call-start = ((), (), s32[]{:S(2)}) async-start(), calls=%async_computation.8 | async-start | bytes 2359296 | tf_op jit(solution)/shard_map/all_gather | solution.py:39
  268.2 11.2 %copy-start.5 = (f32[512,128]{0,1:T(8,128)S(1)}, f32[512,128]{0,1:T(8,128)}, u32[]{:S(2)}) copy-start(f32[512,128]{0,1:T(8,128)} %convolution_bitcast_fusion.2) | copy-start | bytes 786436
  278.1 2.2 copy-start.4
  284.4 2.0 copy-start.1
  287.2 90.8 %all-gather.16.cloned.1.call-start = ((), (), s32[]{:S(2)}) async-start(), calls=%async_computation.5 | async-start | bytes 2162688 | tf_op jit(solution)/shard_map/all_gather | solution.py:39
  324.7 137.4 %all-gather.24.cloned.1.call-start = ((), (), s32[]{:S(2)}) async-start(), calls=%async_computation.9 | async-start | bytes 8650752 | tf_op jit(solution)/shard_map/all_gather | solution.py:39
  404.7 23.7 %copy-start.6 = (f32[512,128]{0,1:T(8,128)S(1)}, f32[512,128]{0,1:T(8,128)}, u32[]{:S(2)}) copy-start(f32[512,128]{0,1:T(8,128)} %convolution_bitcast_fusion.1) | copy-start | bytes 786436
  409.1 18.6 %all-to-all-start.2 = ((f32[8,64,128]{2,1,0:T(8,128)}), f32[8,64,128]{2,1,0:T(8,128)S(1)}, u32[]{:S(2)}, u32[]{:S(2)}) async-start(f32[8,64,128]{2,1,0:T(8,128)} %bitcast.201), calls=%async_computation.2 | async-start | bytes 524288 | tf_op jit(solution)/shard_map/all_to_all | solution.py:34
  472.0 2.2 copy-start.2
Sparse Core Ops, SparseCore 0:
  21.7 53.3 all-gather.11
  99.9 29.2 all-gather.17
  132.3 51.7 all-gather.13
  211.0 57.1 all-gather.19
  287.3 35.8 all-gather.21
  326.2 51.7 all-gather.15
  404.9 57.1 all-gather.23
